TPU v7x, 512 devices: a whole 4x4x16 slice. The times are simulated.
512 devices in a mesh: segment: 2 (over core), seq: 32 (over x, z_lo), mp: 8 (over z_hi, y).
Axes of the slice: x: 4, y: 4, z: 16 (z_hi: 2, z_lo: 8; z = z_hi * 8 + z_lo), core: 2. Of those that a mesh axis runs over, the one named last changes fastest.
Arguments:
- hidden: bfloat16 [2, 2, 5120, 2048], P('segment', None, 'seq', 'mp'), may hold values from -120 to 120
- memory: bfloat16 [2, 2, 5120, 2048], P('segment', None, 'seq', 'mp'), may hold values from -120 to 120
- w_query: bfloat16 [2, 2048, 2048], P('segment', None, 'mp'), may hold values from -1 to 1
- w_key: bfloat16 [2, 2048, 2048], P('segment', None, 'mp'), may hold values from -4 to 4
- w_value: bfloat16 [2, 2048, 2048], P('segment', None, 'mp'), may hold values from -0.125 to 0.125
- w_out: bfloat16 [2, 2048, 2048], P('segment', 'mp'), may hold values from -3 to 3
- norm_gain: float32 [2, 2048], P('segment'), may hold values from 0.1 to 1.9
- final_gain: float32 [2048], replicated, may hold values from 0.1 to 1.9
- lengths: int32 [2, 2, 2], P('segment'), may hold values from 2560 to 5120, as said below
Outputs:
- sublayer: bfloat16 [2, 2, 5120, 2048], P('segment', None, 'seq', 'mp')
Inputs may be any that keep to these rules, and one draw needn't show every extreme that they name: For each sequence b: lengths[0, b, 0] equals lengths[0, b, 1] (the encoder's document length); lengths[1, b, 0] is the target length and lengths[1, b, 1] the length of the document whose memory the decoder reads; one of these three lengths equals 5120.
All inputs are finite; a program needn't handle non-finite values.
Results may differ from a plain program's by a relative error of at most 0.018.
Values may be sent and summed in bfloat16 or wider, within the bound.
A program may use at most 128 MiB of HBM per device.

v0:
```python
import jax
import jax.numpy as jnp
from jax import lax
from jax.sharding import PartitionSpec as P

DH = 64


def passed_along(value, axis, steps):
    count = lax.axis_size(axis)
    leading, last = (max(0, -steps), min(count, count - steps))
    return lax.ppermute(value, axis, [(source, source + steps) for source in range(leading, last)])


def normalize(values, gain_row):
    widened = values.astype(jnp.float32)
    square = jnp.mean(widened * widened, axis=-1, keepdims=True)
    return (widened * lax.rsqrt(square + 1e-06) * gain_row).astype(jnp.bfloat16)


def body(hidden, memory, w_query, w_key, w_value, w_out, norm_gain, final_gain, lengths):
    encoder_side = lax.axis_index("segment") == 0
    own_part = hidden[0]
    arrived = passed_along(memory[0], "segment", 1)
    source_part = jnp.where(encoder_side, own_part, arrived)
    query_rows, source_rows = (
        lax.all_gather(own_part, "mp", axis=2, tiled=True),
        lax.all_gather(source_part, "mp", axis=2, tiled=True),
    )
    batch = own_part.shape[0]
    row_count = own_part.shape[1]
    width = query_rows.shape[2]
    key_gain = jnp.where(encoder_side, norm_gain[0], final_gain)
    query_in = normalize(query_rows.reshape(batch * row_count, width), norm_gain[0])
    key_in = normalize(source_rows.reshape(batch * row_count, width), key_gain)
    head_cols = w_query.shape[2]
    local_heads = head_cols // DH
    queries = jnp.dot(query_in, w_query[0], preferred_element_type=jnp.float32).astype(jnp.bfloat16)
    keys = jnp.dot(key_in, w_key[0], preferred_element_type=jnp.float32).astype(jnp.bfloat16)
    values = jnp.dot(key_in, w_value[0], preferred_element_type=jnp.float32).astype(jnp.bfloat16)
    keys = keys.reshape(batch, row_count, head_cols)
    values = values.reshape(batch, row_count, head_cols)
    query_length = lengths[0, :, 0]
    key_length = lengths[0, :, 1]
    split_queries = queries.reshape(batch, row_count, local_heads, DH)
    key_piece = lax.all_gather(keys, "seq", axis=1, tiled=True)
    value_piece = lax.all_gather(values, "seq", axis=1, tiled=True)
    key_count = key_piece.shape[1]
    running_max = jnp.full((batch, row_count, local_heads), -1e30, jnp.float32)
    scores = (
        jnp.einsum(
            "bqhd,bkhd->bqhk",
            split_queries,
            key_piece.reshape(batch, key_count, local_heads, DH),
            preferred_element_type=jnp.float32,
        )
        * 0.25
    )
    visible = jnp.arange(key_count)[None, :] < key_length[:, None]
    mask = visible[:, None, None, :]
    scores = jnp.where(mask, scores, -1e30)
    new_max = jnp.maximum(running_max, jnp.max(scores, axis=-1))
    exponent = jnp.where(mask, jnp.exp(scores - new_max[..., None]), 0.0)
    totals = jnp.sum(exponent, axis=-1)
    weighted = jnp.einsum(
        "bqhk,bkhd->bqhd",
        exponent.astype(jnp.bfloat16),
        value_piece.reshape(batch, key_count, local_heads, DH),
        preferred_element_type=jnp.float32,
    )
    numerator = weighted
    running_max, totals, numerator = (new_max, totals, numerator)
    context = numerator / totals[..., None]
    positions = lax.axis_index("seq") * row_count + jnp.arange(row_count)
    live_rows = positions[None, :] < query_length[:, None]
    context = jnp.where(live_rows[:, :, None, None], context, 0.0)
    context = context.astype(jnp.bfloat16).reshape(batch * row_count, head_cols)
    partial_value = jnp.dot(context, w_out[0], preferred_element_type=jnp.float32)
    branch = lax.psum_scatter(
        partial_value.astype(jnp.bfloat16), "mp", scatter_dimension=1, tiled=True
    ).astype(jnp.float32)
    branch = branch.reshape(batch, row_count, branch.shape[1])
    return (own_part.astype(jnp.float32) + branch).astype(jnp.bfloat16)[None]


def solution(mesh):
    return jax.shard_map(
        body,
        mesh=mesh,
        in_specs=(
            P("segment", None, "seq", "mp"),
            P("segment", None, "seq", "mp"),
            P("segment", None, "mp"),
            P("segment", None, "mp"),
            P("segment", None, "mp"),
            P("segment", "mp", None),
            P("segment", None),
            P(),
            P("segment", None, None),
        ),
        out_specs=P("segment", None, "seq", "mp"),
        check_vma=False,
    )
```

profile of v0, /device:TPU:6, one launch (start us, length us, event | category | flops | bytes accessed | tf_op | source)
XLA Modules:
  0.0 833.7 jit_solution(6304263238786612045)
XLA Ops:
  6.5 1.9 collective-permute-start
  8.4 1.2 collective-permute-done
  9.6 1.6 bitcast_select_fusion
  11.3 0.7 all-gather.12.cloned.1.call-update
  12.1 0.7 broadcast_select_fusion
  12.8 99.3 %all-gather.6.cloned.1.call-done = bf16[2,160,2048]{2,1,0:T(8,128)(2,1)} async-done(((bf16[2,160,256]{2,1,0:T(8,128)(2,1)}), bf16[2,160,2048]{2,1,0:T(8,128)(2,1)}) %all-gather.6.cloned.1.call-update) | async-done | bytes 1310736 | tf_op jit(solution)/shard_map/all_gather | solution.py:28
  112.1 1.7 fusion.8
  113.7 1.7 fusion.10
  115.4 2.4 convolution_convert_fusion.2
  117.9 0.0 all-gather.8.cloned.1.call-start
  117.9 1.2 convolution_convert_fusion.3
  119.2 0.0 reduce-scatter.2.cloned.1.call-start
  119.2 0.2 slice_reduce_fusion.1
  119.4 0.1 broadcast_compare_fusion
  119.5 0.1 iota_compare_fusion
  119.6 83.3 %all-gather.12.cloned.1.call-done = bf16[1,2,160,2048]{3,2,1,0:T(8,128)(2,1)} async-done(((bf16[1,2,160,256]{3,2,1,0:T(8,128)(2,1)}), bf16[1,2,160,2048]{3,2,1,0:T(8,128)(2,1)}) %all-gather.12.cloned.1.call-update) | async-done | bytes 1310736 | tf_op jit(solution)/shard_map/all_gather | solution.py:27
  202.9 1.7 fusion.11
  204.5 1.7 fusion.13
  206.2 1.8 convolution_convert_fusion.1
  208.0 0.2 reshape.153
  208.2 212.5 %all-gather.10.cloned.1.call-done = bf16[2,5120,256]{2,1,0:T(8,128)(2,1)} async-done(((bf16[2,160,256]{2,1,0:T(8,128)(2,1)}), bf16[2,5120,256]{2,1,0:T(8,128)(2,1)}) %all-gather.10.cloned.1.call-update) | async-done | bytes 5242896 | tf_op jit(solution)/shard_map/all_gather | solution.py:46
  420.7 8.1 copy.14
  428.8 12.3 %bitcast_reduce_fusion = (f32[2,160,4]{1,2,0:T(4,128)S(1)}, f32[2,4,5120,160]{2,3,1,0:T(8,128)}) fusion(pred[2,5120]{1,0:T(4,128)(4,1)S(1)} %iota_compare_fusion, bf16[2,5120,4,64]{1,3,2,0:T(8,128)(2,1)} %bitcast.64, bf16[2,160,4,64]{3,2,1,0:T(4,128)(2,1)S(1)} %reshape.153), kind=kOutput, calls=%fused_computation.1 | convolution fusion | flops 858520320 | bytes 31636480 | tf_op jit(solution)/shard_map/bqhd,bkhd->bqhk/dot_general | solution.py:51
  441.1 10.2 %fusion.2 = f32[2,160,4]{1,2,0:T(4,128)S(1)} fusion(f32[2,4,5120,160]{2,3,1,0:T(8,128)} %get-tuple-element.8, f32[2,160,4]{1,2,0:T(4,128)S(1)} %broadcast_maximum_fusion, pred[2,5120]{1,0:T(4,128)(4,1)S(1)} %iota_compare_fusion), kind=kLoop, calls=%fused_computation.5 | loop fusion | flops 32766720 | bytes 26234880 | tf_op jit(solution)/shard_map/reduce_sum | solution.py:64
  451.4 211.3 %all-gather.8.cloned.1.call-done = bf16[2,5120,256]{2,1,0:T(8,128)(2,1)} async-done(((bf16[2,160,256]{2,1,0:T(8,128)(2,1)}), bf16[2,5120,256]{2,1,0:T(8,128)(2,1)}) %all-gather.8.cloned.1.call-update) | async-done | bytes 5242896 | tf_op jit(solution)/shard_map/all_gather | solution.py:47
  662.7 8.1 copy.13
  670.7 13.1 %fusion.23 = bf16[2,160,4,64]{1,3,2,0:T(8,128)(2,1)S(1)} fusion(bf16[2,5120,4,64]{1,3,2,0:T(8,128)(2,1)} %bitcast.65, f32[2,4,5120,160]{2,3,1,0:T(8,128)} %get-tuple-element.8, f32[2,160,4]{1,2,0:T(4,128)S(1)} %broadcast_maximum_fusion, pred[2,5120]{1,0:T(4,128)(4,1)S(1)} %iota_compare_fusion, f32[2,160,4]{1,2,0:T(4,128)S(1)} %fusion.2, ...), kind=kOutput, calls=%fused_computation.27 | convolution fusion | flops 871874560 | bytes 31641920 | tf_op jit(solution)/shard_map/bqhk,bkhd->bqhd/dot_general | solution.py:65
  683.9 0.3 copy.17
  684.1 0.2 reshape.146
  684.3 1.6 convolution_convert_fusion
  685.9 139.6 %reduce-scatter.2.cloned.1.call-done = bf16[320,256]{1,0:T(8,128)(2,1)} async-done(((bf16[320,2048]{1,0:T(8,128)(2,1)}), bf16[320,256]{1,0:T(8,128)(2,1)}) %reduce-scatter.2.cloned.1.call-update) | async-done | bytes 163856 | tf_op jit(solution)/shard_map/reduce_scatter | solution.py:79
  825.6 1.6 fusion.30
  (21 shorter events, 0.2 us)
Async XLA Ops:
  6.5 677.8 %copy-start = (bf16[1,256,2048]{2,1,0:T(8,128)(2,1)S(1)}, bf16[1,256,2048]{2,1,0:T(8,128)(2,1)}, u32[]{:S(2)}) copy-start(bf16[1,256,2048]{2,1,0:T(8,128)(2,1)} %param.14) | copy-start | bytes 3145732
  6.5 111.4 %copy-start.4 = (bf16[1,2048,256]{2,1,0:T(8,128)(2,1)S(1)}, bf16[1,2048,256]{2,1,0:T(8,128)(2,1)}, u32[]{:S(2)}) copy-start(bf16[1,2048,256]{2,1,0:T(8,128)(2,1)} %param.13) | copy-start | bytes 3145732
  6.5 105.5 %all-gather.6.cloned.1.call-start = ((), (), s32[]{:S(2)}) async-start(), calls=%async_computation.1 | async-start | bytes 1474560 | tf_op jit(solution)/shard_map/all_gather | solution.py:28
  6.5 3.1 collective-permute-start
  11.3 191.6 %all-gather.12.cloned.1.call-start = ((), (), s32[]{:S(2)}) async-start(), calls=%async_computation.5 | async-start | bytes 1474560 | tf_op jit(solution)/shard_map/all_gather | solution.py:27
  12.0 408.7 %all-gather.10.cloned.1.call-start = ((), (), s32[]{:S(2)}) async-start(), calls=%async_computation.3 | async-start | bytes 5406720 | tf_op jit(solution)/shard_map/all_gather | solution.py:46
  113.7 5.5 copy-start.3
  115.4 89.1 %copy-start.2 = (f32[1,2048]{1,0:T(1,128)S(1)}, f32[1,2048]{1,0:T(1,128)}, u32[]{:S(2)}) copy-start(f32[1,2048]{1,0:T(1,128)} %param.15) | copy-start | bytes 24580
  117.9 544.8 %all-gather.8.cloned.1.call-start = ((), (), s32[]{:S(2)}) async-start(), calls=%async_computation.2 | async-start | bytes 5406720 | tf_op jit(solution)/shard_map/all_gather | solution.py:47
  119.2 706.4 %reduce-scatter.2.cloned.1.call-start = ((), (), s32[]{:S(2)}) async-start(), calls=%async_computation.4 | async-start | bytes 1474560 | tf_op jit(solution)/shard_map/reduce_scatter | solution.py:79
  670.7 154.8 %copy-start.1 = (bf16[1,2,160,256]{3,2,1,0:T(8,128)(2,1)S(1)}, bf16[1,2,160,256]{3,2,1,0:T(8,128)(2,1)}, u32[]{:S(2)}) copy-start(bf16[1,2,160,256]{3,2,1,0:T(8,128)(2,1)} %param.9) | copy-start | bytes 491524
Sparse Core Ops, SparseCore 0:
  11.4 100.6 all-gather.5
  115.1 87.7 all-gather.11
  205.0 215.7 all-gather.9
  422.7 239.9 all-gather.7
  686.1 139.4 reduce-scatter.1
where the time goes:
time: 835 us; the launch traced here: 834 us
  waiting for transfers between devices  748 us (90%)
  matrix products  32.4 us (4%)
  other arithmetic  21 us (3%)
  local copies, waits for them, and re-layouts  16.9 us (2%)
  between operations  13.3 us (2%)
    all_gather x1, waiting for transfers between devices, body(): key_piece = lax.all_gather(keys, 'seq', axis=1, tiled=True)  213 us
    all_gather x1, waiting for transfers between devices, body(): value_piece = lax.all_gather(values, 'seq', axis=1, tiled=True)  211 us
    reduce_scatter x1, waiting for transfers between devices, body(): lax.psum_scatter(partial_value.astype(jnp.bfloat16), 'mp', scatter_dimens...  140 us
    all_gather x1, waiting for transfers between devices, body(): lax.all_gather(source_part, 'mp', axis=2, tiled=True)  99.3 us
    all_gather x1, waiting for transfers between devices, body(): lax.all_gather(own_part, 'mp', axis=2, tiled=True)  83.3 us
  transfers between devices with their start and end apart: 6, of which 6 were waited for; matrix products, arithmetic and copies ran while one was open for 5% of the time, Pallas kernels for 0%

commit v1 on v0

v1 whole, which is shorter than its diff:
```python
import functools
import math

import jax
import jax.numpy as jnp
from jax import lax
from jax.experimental import pallas as pl
from jax.experimental.pallas import tpu as pltpu
from jax.sharding import PartitionSpec as P

DH = 64
NX, NZ, NH, NY = 4, 8, 2, 4
LANES = 128
BF = jnp.bfloat16
F32 = jnp.float32
VMEM_LIMIT = 48 * 1024 * 1024


def place():
    seg, seq, mp = lax.axis_index("segment"), lax.axis_index("seq"), lax.axis_index("mp")
    return seg, seq // NZ, seq % NZ, mp // NY, mp % NY


def at(seg, x, zl, zh, y):
    return (seg, x * NZ + zl, zh * NY + y)


def push(src, dst, send, recv, device):
    return pltpu.make_async_remote_copy(
        src_ref=src, dst_ref=dst, send_sem=send, recv_sem=recv,
        device_id=device, device_id_type=pl.DeviceIdType.MESH,
    )


def greet(partners):
    barrier = pltpu.get_barrier_semaphore()
    for device in partners:
        pl.semaphore_signal(barrier, inc=1, device_id=device, device_id_type=pl.DeviceIdType.MESH)
    pl.semaphore_wait(barrier, len(partners))


def low_lanes(shape):
    return lax.broadcasted_iota(jnp.int32, shape, 1) < DH


def swap(tile):
    return pltpu.roll(tile, DH, 1)


def merge(low, high):
    return jnp.where(low_lanes(low.shape), low, high)


def gather_kernel(
    h_ref, m_ref, wq_ref, wk_ref, wv_ref, gain_ref,
    qa_ref, kva_ref,
    xs, qs, kvs, accq, acck, accv, ssq,
    own_send, mem_send, fwd_send, x_recv, z_send, z_recv, kv_send, kv_recv,
):
    seg, x, zl, zh, y = place()
    mp = zh * NY + y
    other = (NH - 1 - zh) * NY + y
    total, chunk = h_ref.shape
    rows = kvs.shape[1]
    batch = total // rows
    heads = accq.shape[1] // DH
    width = chunk * NH * NY

    here = [(zh, (y + k) % NY) for k in range(1, NY)]
    group = [(NH - 1 - zh, y)] + here
    partners = [at(seg, x, zl, a, b) for a, b in group]
    partners += [at(1 - seg, x, zl, a, b) for a, b in group] + [at(1 - seg, x, zl, zh, y)]
    partners += [at(seg, x, (zl + k) % NZ, zh, y) for k in range(1, NZ)]
    partners += [at(seg, (x + k) % NX, zl, zh, y) for k in range(1, NX)]
    greet(partners)

    def own_copies():
        return [
            push(h_ref, xs.at[0, mp], own_send.at[k], x_recv.at[0, mp], at(seg, x, zl, a, b))
            for k, (a, b) in enumerate(group)
        ]

    def memory_copies():
        return [
            push(m_ref, xs.at[1, mp], mem_send.at[k], x_recv.at[1, mp], at(1, x, zl, a, b))
            for k, (a, b) in enumerate(group + [(zh, y)])
        ]

    def forwards(array):
        return [
            push(xs.at[array, other], xs.at[array, other], fwd_send.at[array, k], x_recv.at[array, other],
                 at(seg, x, zl, a, b))
            for k, (a, b) in enumerate(here)
        ]

    def arrived(array, c):
        push(xs.at[array, c], xs.at[array, c], fwd_send.at[array, 0], x_recv.at[array, c],
             at(seg, x, zl, zh, y)).wait_recv()

    for copy in own_copies():
        copy.start()

    @pl.when(seg == 0)
    def _():
        for copy in memory_copies():
            copy.start()

    xs[0, mp] = h_ref[...]
    accq[...] = jnp.zeros_like(accq)
    acck[...] = jnp.zeros_like(acck)
    accv[...] = jnp.zeros_like(accv)
    ssq[...] = jnp.zeros_like(ssq)

    def chunk_step(j, carry):
        c = (zh + j // NY) % NH * NY + (y + j % NY) % NY

        @pl.when(j > 0)
        def _():
            arrived(0, c)

        @pl.when(j == NY)
        def _():
            for copy in forwards(0):
                copy.start()

        @pl.when(seg == 1)
        def _():
            arrived(1, c)

            @pl.when(j == NY)
            def _():
                for copy in forwards(1):
                    copy.start()

        cols = pl.ds(pl.multiple_of(c * chunk, chunk), chunk)
        xq = xs[0, c].astype(F32)
        ssq[0] += jnp.sum(xq * xq, axis=1, keepdims=True)
        accq[...] += jnp.dot(
            (xq * gain_ref[0:1, cols]).astype(BF), wq_ref[cols, :], preferred_element_type=F32
        )
        xk = xs[seg, c].astype(F32)
        ssq[1] += jnp.sum(xk * xk, axis=1, keepdims=True)
        xk = (xk * gain_ref[1:2, cols]).astype(BF)
        acck[...] += jnp.dot(xk, wk_ref[cols, :], preferred_element_type=F32)
        accv[...] += jnp.dot(xk, wv_ref[cols, :], preferred_element_type=F32)
        return carry

    lax.fori_loop(0, NH * NY, chunk_step, 0)

    rq = lax.rsqrt(ssq[0, :, 0:1] / width + 1e-06)
    rk = lax.rsqrt(ssq[1, :, 0:1] / width + 1e-06)
    half = rows // 2
    for b in range(batch):
        span = slice(b * rows, (b + 1) * rows)
        for t in range(heads // 2):
            tile = slice(t * LANES, (t + 1) * LANES)
            k = acck[span, tile] * rk[span]
            v = accv[span, tile] * rk[span]
            q = accq[span, tile] * rq[span]
            first = b * heads + 2 * t
            kvs[first] = merge(k, swap(v)).astype(BF)
            kvs[first + 1] = merge(swap(k), v).astype(BF)
            qs[first] = merge(q[:half], swap(q[half:])).astype(BF)
            qs[first + 1] = merge(swap(q[:half]), q[half:]).astype(BF)

    def z_copies(k):
        z = (zl + k) % NZ
        device = at(seg, x, z, zh, y)
        return (
            push(kvs.at[z], kva_ref.at[x, zl], z_send.at[0, k], kv_recv.at[x, zl], device),
            push(qs.at[z], qa_ref.at[zl], z_send.at[1, k], z_recv.at[zl], device),
        )

    def z_start(k, carry):
        for copy in z_copies(k):
            copy.start()
        return carry

    lax.fori_loop(1, NZ, z_start, 0)
    kva_ref[x, zl] = kvs[zl]
    qa_ref[zl] = qs[zl]

    def x_copy(k, z):
        return push(kva_ref.at[x, z], kva_ref.at[x, z], kv_send.at[k, z], kv_recv.at[x, z],
                    at(seg, (x + k) % NX, zl, zh, y))

    def kv_arrived(xx, z):
        push(kva_ref.at[xx, z], kva_ref.at[xx, z], kv_send.at[0, 0], kv_recv.at[xx, z],
             at(seg, x, zl, zh, y)).wait_recv()

    def x_start(k, carry):
        z = (zl + NZ - k) % NZ

        @pl.when(k > 0)
        def _():
            kv_arrived(x, z)

        for step in range(1, NX):
            x_copy(step, z).start()
        return carry

    lax.fori_loop(0, NZ, x_start, 0)

    def x_wait(k, carry):
        z = (zl + NZ - k) % NZ
        for step in range(1, NX):
            kv_arrived((x + step) % NX, z)

        @pl.when(k > 0)
        def _():
            push(qa_ref.at[z], qa_ref.at[z], z_send.at[1, 0], z_recv.at[z], at(seg, x, zl, zh, y)).wait_recv()
            for copy in z_copies(k):
                copy.wait_send()

        for step in range(1, NX):
            x_copy(step, z).wait_send()
        return carry

    lax.fori_loop(0, NZ, x_wait, 0)

    for copy in own_copies() + forwards(0):
        copy.wait_send()

    @pl.when(seg == 0)
    def _():
        for copy in memory_copies():
            copy.wait_send()

    @pl.when(seg == 1)
    def _():
        for copy in forwards(1):
            copy.wait_send()


def gather(hidden, memory, w_query, w_key, w_value, gains, rows):
    total, chunk = hidden.shape
    cols = w_query.shape[1]
    parts = NH * NY
    dma = pltpu.SemaphoreType.DMA
    vmem = pl.BlockSpec(memory_space=pltpu.VMEM)
    return pl.pallas_call(
        gather_kernel,
        out_shape=(
            jax.ShapeDtypeStruct((NZ, rows // 2, LANES), BF),
            jax.ShapeDtypeStruct((NX, NZ, rows, LANES), BF),
        ),
        in_specs=[vmem] * 6,
        out_specs=(vmem, vmem),
        scratch_shapes=[
            pltpu.VMEM((2, parts, total, chunk), BF),
            pltpu.VMEM((NZ, rows // 2, LANES), BF),
            pltpu.VMEM((NZ, rows, LANES), BF),
            pltpu.VMEM((total, cols), F32),
            pltpu.VMEM((total, cols), F32),
            pltpu.VMEM((total, cols), F32),
            pltpu.VMEM((2, total, LANES), F32),
            dma((NY,)),
            dma((NY + 1,)),
            dma((2, NY)),
            dma((2, parts)),
            dma((2, NZ)),
            dma((NZ,)),
            dma((NX, NZ)),
            dma((NX, NZ)),
        ],
        compiler_params=pltpu.CompilerParams(
            collective_id=1, has_side_effects=True, vmem_limit_bytes=VMEM_LIMIT
        ),
        name="gather",
    )(hidden, memory, w_query, w_key, w_value, gains)


def attend_kernel(limits, qa_ref, kv_ref, out_ref, keys, scores):
    step = pl.program_id(0)
    count = kv_ref.shape[0]
    sources, half, _ = qa_ref.shape
    block = scores.shape[0]
    pieces = 5

    @pl.when(step == 0)
    def _():
        keys[:, :LANES] = kv_ref[...]
        row = lax.broadcasted_iota(jnp.int32, (count, LANES), 0)
        lane = lax.broadcasted_iota(jnp.int32, (count, LANES), 1)
        bias = jnp.where(row < limits[1], 0.0, -1e30)
        keys[:, LANES:] = jnp.where(lane == 0, bias, jnp.where(lane == 1, 1.0, 0.0)).astype(BF)

    parts = []
    for s in range(sources):
        packed = qa_ref[s].astype(F32)
        parts += [merge(packed, jnp.zeros_like(packed)), merge(swap(packed), jnp.zeros_like(packed))]
    query = jnp.concatenate(parts, axis=0).astype(BF)
    flag = (lax.broadcasted_iota(jnp.int32, (block, LANES), 1) == 0).astype(BF)
    query = jnp.concatenate([query, flag], axis=1)

    size = count // pieces
    top = None
    for i in range(pieces):
        part = lax.dot_general(
            query, keys[i * size:(i + 1) * size, :], (((1,), (1,)), ((), ())), preferred_element_type=F32
        )
        scores[:, i * size:(i + 1) * size] = part
        high = jnp.max(part, axis=1, keepdims=True)
        top = high if top is None else jnp.maximum(top, high)
    factor = 0.25 / math.log(2.0)
    shift = top * factor
    acc = None
    for i in range(pieces):
        weight = jnp.exp2(scores[:, i * size:(i + 1) * size] * factor - shift).astype(BF)
        part = jnp.dot(weight, keys[i * size:(i + 1) * size, :], preferred_element_type=F32)
        acc = part if acc is None else acc + part
    context = acc[:, :LANES] / acc[:, LANES + 1:LANES + 2]
    first = limits[2] + step * block
    position = first + lax.broadcasted_iota(jnp.int32, (block, LANES), 0)
    context = jnp.where(position < limits[0], context, 0.0)
    for s in range(sources):
        low = context[2 * s * half:(2 * s + 1) * half]
        high = context[(2 * s + 1) * half:(2 * s + 2) * half]
        out_ref[s] = merge(swap(low), high).astype(BF)


def attend(limits, queries, keys):
    count = keys.shape[0]
    places, half, _ = queries.shape
    sources = 2
    block = 2 * half * sources
    return pl.pallas_call(
        attend_kernel,
        out_shape=jax.ShapeDtypeStruct(queries.shape, BF),
        grid_spec=pltpu.PrefetchScalarGridSpec(
            num_scalar_prefetch=1,
            grid=(places // sources,),
            in_specs=[
                pl.BlockSpec((sources, half, LANES), lambda i, _: (i, 0, 0)),
                pl.BlockSpec((count, LANES), lambda i, _: (0, 0)),
            ],
            out_specs=pl.BlockSpec((sources, half, LANES), lambda i, _: (i, 0, 0)),
            scratch_shapes=[pltpu.VMEM((count, 2 * LANES), BF), pltpu.VMEM((block, count), F32)],
        ),
        compiler_params=pltpu.CompilerParams(vmem_limit_bytes=VMEM_LIMIT),
        name="attend",
    )(limits, queries, keys)


def output_kernel(
    ctx_ref, w_ref, h_ref, out_ref,
    back, full, part, own, landed, z_out, z_in,
    c_send, c_recv, y_send, y_recv, h_send, h_recv,
):
    seg, x, zl, zh, y = place()
    far = NH - 1 - zh
    total, chunk = h_ref.shape
    half = back.shape[1]
    rows = 2 * half
    batch = total // rows
    heads = w_ref.shape[0] // DH

    partners = [at(seg, x, (zl + k) % NZ, zh, y) for k in range(1, NZ)]
    partners += [at(seg, x, zl, zh, (y + k) % NY) for k in range(1, NY)] + [at(seg, x, zl, far, y)]
    greet(partners)

    def z_copy(k):
        z = (zl + k) % NZ
        return push(ctx_ref.at[z], back.at[zl], c_send.at[k], c_recv.at[zl], at(seg, x, z, zh, y))

    def z_start(k, carry):
        z_copy(k).start()
        return carry

    lax.fori_loop(1, NZ, z_start, 0)
    back[zl] = ctx_ref[zl]

    def z_wait(k, carry):
        z = (zl + NZ - k) % NZ
        push(back.at[z], back.at[z], c_send.at[0], c_recv.at[z], at(seg, x, zl, zh, y)).wait_recv()
        z_copy(k).wait_send()
        return carry

    lax.fori_loop(1, NZ, z_wait, 0)
    for b in range(batch):
        for t in range(heads // 2):
            even = back[b * heads + 2 * t].astype(F32)
            odd = back[b * heads + 2 * t + 1].astype(F32)
            tile = slice(t * LANES, (t + 1) * LANES)
            full[b * rows:b * rows + half, tile] = merge(even, swap(odd)).astype(BF)
            full[b * rows + half:(b + 1) * rows, tile] = merge(swap(even), odd).astype(BF)

    def projected(zz, yy):
        cols = pl.ds(pl.multiple_of((zz * NY + yy) * chunk, chunk), chunk)
        return jnp.dot(full[...], w_ref[:, cols], preferred_element_type=F32)

    def y_copy(k):
        yy = (y + k) % NY
        return push(part.at[yy], landed.at[y], y_send.at[k], y_recv.at[y], at(seg, x, zl, zh, yy))

    def y_start(k, carry):
        yy = (y + k) % NY
        for zz in range(NH):
            part[yy, zz] = projected(zz, yy).astype(BF)
        y_copy(k).start()
        return carry

    lax.fori_loop(1, NY, y_start, 0)
    for zz in range(NH):
        own[zz] = projected(zz, y)

    def y_wait(k, carry):
        yy = (y + NY - k) % NY
        push(landed.at[yy], landed.at[yy], y_send.at[0], y_recv.at[yy], at(seg, x, zl, zh, y)).wait_recv()
        for zz in range(NH):
            own[zz] += landed[yy, zz].astype(F32)
        return carry

    lax.fori_loop(1, NY, y_wait, 0)
    z_out[...] = own[far].astype(BF)
    exchange = push(z_out, z_in, h_send, h_recv, at(seg, x, zl, far, y))
    exchange.start()
    exchange.wait()
    out_ref[...] = (h_ref[...].astype(F32) + own[zh] + z_in[...].astype(F32)).astype(BF)
    for k in range(1, NY):
        y_copy(k).wait_send()


def output(context, w_out, hidden):
    total, chunk = hidden.shape
    places, half, _ = context.shape
    cols = w_out.shape[0]
    dma = pltpu.SemaphoreType.DMA
    vmem = pl.BlockSpec(memory_space=pltpu.VMEM)
    return pl.pallas_call(
        output_kernel,
        out_shape=jax.ShapeDtypeStruct((total, chunk), BF),
        in_specs=[vmem] * 3,
        out_specs=vmem,
        scratch_shapes=[
            pltpu.VMEM((places, half, LANES), BF),
            pltpu.VMEM((total, cols), BF),
            pltpu.VMEM((NY, NH, total, chunk), BF),
            pltpu.VMEM((NH, total, chunk), F32),
            pltpu.VMEM((NY, NH, total, chunk), BF),
            pltpu.VMEM((total, chunk), BF),
            pltpu.VMEM((total, chunk), BF),
            dma((NZ,)),
            dma((NZ,)),
            dma((NY,)),
            dma((NY,)),
            dma(()),
            dma(()),
        ],
        compiler_params=pltpu.CompilerParams(
            collective_id=2, has_side_effects=True, vmem_limit_bytes=VMEM_LIMIT
        ),
        name="output",
    )(context, w_out, hidden)


def body(hidden, memory, w_query, w_key, w_value, w_out, norm_gain, final_gain, lengths):
    seg, x, zl, _, _ = place()
    _, batch, rows, chunk = hidden.shape
    heads = w_query.shape[2] // DH
    own = hidden[0].reshape(batch * rows, chunk)
    mem = memory[0].reshape(batch * rows, chunk)
    gains = jnp.stack([norm_gain[0], jnp.where(seg == 0, norm_gain[0], final_gain)])
    queries, keys = gather(own, mem, w_query[0], w_key[0], w_value[0], gains, rows)
    pair = lax.dynamic_index_in_dim(lengths[0], zl // heads, 0, keepdims=False)
    limits = jnp.concatenate([pair, jnp.array([x * NZ * rows], jnp.int32)])
    context = attend(limits, queries, keys.reshape(NX * NZ * rows, LANES))
    out = output(context, w_out[0], own)
    return out.reshape(1, batch, rows, chunk)


def solution(mesh):
    return jax.shard_map(
        body,
        mesh=mesh,
        in_specs=(
            P("segment", None, "seq", "mp"),
            P("segment", None, "seq", "mp"),
            P("segment", None, "mp"),
            P("segment", None, "mp"),
            P("segment", None, "mp"),
            P("segment", "mp", None),
            P("segment", None),
            P(),
            P("segment", None, None),
        ),
        out_specs=P("segment", None, "seq", "mp"),
        check_vma=False,
    )
```

time: 835 us -> 157 us (0.19)
  the two profiles are of different devices: /device:TPU:6 before, /device:TPU:32 now
where the time goes in v1:
time: 157 us
  Pallas kernels  149 us (95%)
  local copies, waits for them, and re-layouts  6.86 us (4%)
    pallas_call x1, Pallas kernels, gather(): pl.pallas_call(gather_kernel, out_shape=(jax.ShapeDtypeStruct((NZ, rows /...  68.8 us
    pallas_call x1, Pallas kernels, output(): pl.pallas_call(output_kernel, out_shape=jax.ShapeDtypeStruct((total, chun...  59.1 us
    pallas_call x1, Pallas kernels, attend(): pl.pallas_call(attend_kernel, out_shape=jax.ShapeDtypeStruct(queries.shap...  20.8 us
    unnamed x17, local copies, waits for them, and re-layouts  6.86 us

profile of v1, /device:TPU:32, one launch (start us, length us, event | category | flops | bytes accessed | tf_op | source)
XLA Modules:
  0.0 157.1 jit_solution(12550841207867432068)
XLA Ops:
  0.0 0.0 copy-start
  0.0 0.7 copy-done
  0.7 0.1 pad_add_fusion.limits
  0.8 0.7 broadcast_select_fusion
  1.5 0.7 pad_maximum_fusion.gain_ref
  2.2 0.0 copy-start.2
  2.2 1.2 copy-done.2
  3.4 0.0 copy-start.3
  3.4 1.2 copy-done.3
  4.6 0.0 copy-start.4
  4.6 1.2 copy-done.4
  5.9 0.0 copy-start.5
  5.9 0.9 copy-done.5
  6.8 0.0 copy-start.7
  6.8 0.9 copy-done.7
  7.7 68.8 %gather.1 = (bf16[8,80,128]{2,1,0:T(8,128)(2,1)S(1)}, bf16[4,8,160,128]{3,2,1,0:T(8,128)(2,1)S(1)}) custom-call(bf16[320,256]{1,0:T(8,128)(2,1)S(1)} %bitcast.19, bf16[320,256]{1,0:T(8,128)(2,1)S(1)} %bitcast.21, bf16[2048,256]{1,0:T(8,128)(2,1)S(1)} %bitcast.15, bf16[2048,256]{1,0:T(8,128)(2,1)S(1)} %bitcast.16, bf16[2048,256]{1,0:T(8,128)(2,1)S(1)} %bitcast.17, ...), custom_call_target="tpu_custom_call" | custom-call | tf_op jit(solution)/shard_map/gather/pallas_call | solution.py:241
  76.5 0.0 copy-start.1
  76.5 0.0 copy-start.6
  76.5 20.8 %attend.1.ctx_ref = bf16[8,80,128]{2,1,0:T(8,128)(2,1)S(1)} custom-call(s32[3]{0:T(128)S(1)} %pad_add_fusion.limits, bf16[8,80,128]{2,1,0:T(8,128)(2,1)S(1)} %get-tuple-element.7.qa_ref, bf16[5120,128]{1,0:T(8,128)(2,1)S(1)} %bitcast.13), custom_call_target="tpu_custom_call" | custom-call | tf_op jit(solution)/shard_map/attend/pallas_call | solution.py:327
  97.3 0.0 copy-done.1
  97.3 0.0 copy-done.6
  97.3 59.1 %output.1 = bf16[320,256]{1,0:T(8,128)(2,1)S(1)} custom-call(bf16[8,80,128]{2,1,0:T(8,128)(2,1)S(1)} %attend.1.ctx_ref, bf16[256,2048]{1,0:T(8,128)(2,1)S(1)} %bitcast.14, bf16[320,256]{1,0:T(8,128)(2,1)S(1)} %bitcast.20), custom_call_target="tpu_custom_call" | custom-call | tf_op jit(solution)/shard_map/output/pallas_call | solution.py:430
  156.4 0.7 copy.11
  (1 shorter events, 0.0 us)
Async XLA Ops:
  0.0 0.7 copy-start
  2.2 1.2 copy-start.2
  3.4 1.2 copy-start.3
  4.6 1.2 copy-start.4
  5.9 0.9 copy-start.5
  6.8 0.9 copy-start.7
  76.5 20.8 %copy-start.1 = (bf16[1,256,2048]{2,1,0:T(8,128)(2,1)S(1)}, bf16[1,256,2048]{2,1,0:T(8,128)(2,1)}, u32[]{:S(2)}) copy-start(bf16[1,256,2048]{2,1,0:T(8,128)(2,1)} %param.14) | copy-start | bytes 3145732
  76.5 20.8 %copy-start.6 = (bf16[1,2,160,256]{3,2,1,0:T(8,128)(2,1)S(1)}, bf16[1,2,160,256]{3,2,1,0:T(8,128)(2,1)}, u32[]{:S(2)}) copy-start(bf16[1,2,160,256]{3,2,1,0:T(8,128)(2,1)} %param.9) | copy-start | bytes 491524

commit v2 on v0

v2 whole, which is shorter than its diff:
```python
import math

import jax
import jax.numpy as jnp
from jax import lax
from jax.experimental import pallas as pl
from jax.experimental.pallas import tpu as pltpu
from jax.sharding import PartitionSpec as P

DH = 64
NX, NZ, NH, NY = 4, 8, 2, 4
PIECES = 5
LANES = 128
BF = jnp.bfloat16
F32 = jnp.float32
VMEM_LIMIT = 56 * 1024 * 1024
EARLY, LATE = 0, 1


def place():
    seg, seq, mp = lax.axis_index("segment"), lax.axis_index("seq"), lax.axis_index("mp")
    return seg, seq // NZ, seq % NZ, mp // NY, mp % NY


def at(seg, x, zl, zh, y):
    return (seg, x * NZ + zl, zh * NY + y)


def push(src, dst, send, recv, device):
    return pltpu.make_async_remote_copy(
        src_ref=src, dst_ref=dst, send_sem=send, recv_sem=recv,
        device_id=device, device_id_type=pl.DeviceIdType.MESH,
    )


def greet(partners):
    barrier = pltpu.get_barrier_semaphore()
    for device in partners:
        pl.semaphore_signal(barrier, inc=1, device_id=device, device_id_type=pl.DeviceIdType.MESH)
    pl.semaphore_wait(barrier, len(partners))


def swap(tile):
    return pltpu.roll(tile, DH, 1)


def merge(low, high):
    return jnp.where(lax.broadcasted_iota(jnp.int32, low.shape, 1) < DH, low, high)


def layer_kernel(
    lengths_ref, h_ref, m_ref, wq_hbm, wk_hbm, wv_hbm, wo_hbm, norm_ref, final_ref,
    out_ref,
    hv, wq, wk, wv, wo, gain, xs, accq, acck, accv, ssq, qs, kvs, qa, kva, aux, scores,
    co, back, full, part, own, landed, fs, fin,
    local, z_send, f_send, x_recv, a_send, q_recv, kv_recv, xf_send, c_send, c_recv, y_send, y_recv,
    e_send, e_recv,
):
    seg, x, zl, zh, y = place()
    nc = NZ // 2
    cb, zi = zl // nc, zl % nc
    z4 = (zl + nc) % NZ
    far = NH - 1 - zh
    mp, omp = zh * NY + y, far * NY + y
    batch, rows, chunk = hv.shape
    half = rows // 2
    heads = nc
    width = chunk * NH * NY
    count = NX * NZ * rows
    me = at(seg, x, zl, zh, y)

    loads = [
        pltpu.make_async_copy(src, dst, local.at[i])
        for i, (src, dst) in enumerate(
            [(h_ref, hv), (wq_hbm, wq), (wk_hbm, wk), (wv_hbm, wv), (wo_hbm, wo)]
        )
    ]
    for load in loads:
        load.start()

    partners = [at(seg, x, zl, far, y), at(seg, x, z4, zh, y), at(seg, x, z4, far, y)]
    partners += [at(1 - seg, x, a, b, y) for a, b in [(zl, zh), (zl, far), (z4, zh), (z4, far)]]
    partners += [at(seg, x, zl, zh, (y + k) % NY) for k in range(1, NY)]
    partners += [at(seg, x, cb * nc + (zi + k) % nc, zh, y) for k in range(1, nc)]
    partners += [at(seg, (x + k) % NX, zl, zh, y) for k in range(1, NX)]
    greet(partners)

    def spread(array, src):
        to = array if array else seg
        targets = [
            (EARLY, at(to, x, z4, zh, y)),
            (EARLY, at(to, x, z4, far, y)),
            (LATE, at(to, x, zl, far, y)),
        ]
        if array:
            targets.append((LATE, at(to, x, zl, zh, y)))
        return [
            push(src.at[(cb + 1 - rb) % 2], xs.at[array, rb, mp], z_send.at[array, i], x_recv.at[array, rb, mp], d)
            for i, (rb, d) in enumerate(targets)
        ]

    def arrived(array, rb, c):
        push(xs.at[array, rb, c], xs.at[array, rb, c], f_send.at[0, 0, 0], x_recv.at[array, rb, c], me).wait_recv()

    def along_y(array, rb, c):
        slot = rb * NH + (0 if c is mp else 1)
        return [
            push(xs.at[array, rb, c], xs.at[array, rb, c], f_send.at[array, slot, k], x_recv.at[array, rb, c],
                 at(seg, x, zl, zh, (y + k) % NY))
            for k in range(1, NY)
        ]

    def forward(array, rb, c, wait=True):
        if wait:
            arrived(array, rb, c)
        for copy in along_y(array, rb, c):
            copy.start()

    def both(rb, c):
        forward(0, rb, c)

        @pl.when(seg == 1)
        def _():
            forward(1, rb, c)

    for copy in spread(0, h_ref):
        copy.start()

    @pl.when(seg == 0)
    def _():
        for copy in spread(1, m_ref):
            copy.start()

    loads[0].wait()
    xs[0, LATE, mp] = hv[cb]
    forward(0, LATE, mp, wait=False)

    @pl.when(seg == 1)
    def _():
        forward(1, LATE, mp)

    gain[0:1, :] = norm_ref[...]
    gain[1:2, :] = jnp.where(seg == 0, norm_ref[...], final_ref[...])
    key_length = lengths_ref[cb, 1]

    def fill(i, carry):
        span = pl.ds(pl.multiple_of(i * rows, rows), rows)
        row = i * rows + lax.broadcasted_iota(jnp.int32, (rows, LANES), 0)
        lane = lax.broadcasted_iota(jnp.int32, (rows, LANES), 1)
        bias = jnp.where(row < key_length, 0.0, -1e30)
        aux[span, :] = jnp.where(lane == 0, bias, jnp.where(lane == 1, 1.0, 0.0)).astype(BF)
        return carry

    lax.fori_loop(0, NX * NZ, fill, 0)
    accq[...] = jnp.zeros_like(accq)
    acck[...] = jnp.zeros_like(acck)
    accv[...] = jnp.zeros_like(accv)
    ssq[...] = jnp.zeros_like(ssq)
    for load in loads[1:4]:
        load.wait()

    def squares(values):
        values = values * values
        return sum(values[:, i * LANES:(i + 1) * LANES] for i in range(chunk // LANES))

    def absorb(rb, first, last):
        def step(j, carry):
            c = (zh + j // NY) % NH * NY + (y + j % NY) % NY

            @pl.when(j % NY > 0)
            def _():
                arrived(0, rb, c)

                @pl.when(seg == 1)
                def _():
                    arrived(1, rb, c)

            cols = pl.ds(pl.multiple_of(c * chunk, chunk), chunk)
            xq = xs[0, rb, c].astype(F32)
            ssq[0, rb] += squares(xq)
            accq[rb] += jnp.dot((xq * gain[0:1, cols]).astype(BF), wq[cols, :], preferred_element_type=F32)
            xk = xs[seg, rb, c].astype(F32)
            ssq[1, rb] += squares(xk)
            xk = (xk * gain[1:2, cols]).astype(BF)
            acck[rb] += jnp.dot(xk, wk[cols, :], preferred_element_type=F32)
            accv[rb] += jnp.dot(xk, wv[cols, :], preferred_element_type=F32)
            return carry

        lax.fori_loop(first, last, step, 0)

    zpos = [z4, zl]

    def kv_slot(xx, z):
        return kva.at[pl.ds(pl.multiple_of((xx * NZ + z) * rows, rows), rows)]

    def exchange(rb, k):
        h = (zi + k) % nc
        device = at(seg, x, cb * nc + h, zh, y)
        return (
            push(kvs.at[rb, h], kv_slot(x, zpos[rb]), a_send.at[rb, 0, k], kv_recv.at[x, zpos[rb]], device),
            push(qs.at[rb, h], qa.at[zpos[rb]], a_send.at[rb, 1, k], q_recv.at[zpos[rb]], device),
        )

    def along_x(z, k):
        return push(kv_slot(x, z), kv_slot(x, z), xf_send.at[z, k], kv_recv.at[x, z], at(seg, (x + k) % NX, zl, zh, y))

    def kv_arrived(xx, z):
        push(kv_slot(xx, z), kv_slot(xx, z), xf_send.at[0, 0], kv_recv.at[xx, z], me).wait_recv()

    def project(rb):
        rq = lax.rsqrt(jnp.sum(ssq[0, rb], axis=1, keepdims=True) / width + 1e-06)
        rk = lax.rsqrt(jnp.sum(ssq[1, rb], axis=1, keepdims=True) / width + 1e-06)
        for t in range(heads // 2):
            tile = slice(t * LANES, (t + 1) * LANES)
            k = acck[rb, :, tile] * rk
            v = accv[rb, :, tile] * rk
            q = accq[rb, :, tile] * rq
            kvs[rb, 2 * t] = merge(k, swap(v)).astype(BF)
            kvs[rb, 2 * t + 1] = merge(swap(k), v).astype(BF)
            qs[rb, 2 * t] = merge(q[:half], swap(q[half:])).astype(BF)
            qs[rb, 2 * t + 1] = merge(swap(q[:half]), q[half:]).astype(BF)
        for k in range(1, nc):
            for copy in exchange(rb, k):
                copy.start()
        kva[pl.ds(pl.multiple_of((x * NZ + zpos[rb]) * rows, rows), rows), :] = kvs[rb, zi]
        qa[zpos[rb]] = qs[rb, zi]

    def from_z(rb, k):
        return ((cb + 1 - rb) % 2) * nc + (zi + nc - k) % nc

    def pass_x(rb):
        def step(k, carry):
            z = from_z(rb, k)

            @pl.when(k > 0)
            def _():
                kv_arrived(x, z)

            for i in range(1, NX):
                along_x(z, i).start()
            return carry

        lax.fori_loop(0, nc, step, 0)

    absorb(LATE, 0, NY)
    both(EARLY, mp)
    both(EARLY, omp)
    absorb(EARLY, 0, NH * NY)
    project(EARLY)
    both(LATE, omp)
    pass_x(EARLY)
    absorb(LATE, NY, NH * NY)
    project(LATE)
    pass_x(LATE)

    def collect(rb):
        def step(k, carry):
            z = from_z(rb, k)
            for i in range(1, NX):
                kv_arrived((x + i) % NX, z)

            @pl.when(k > 0)
            def _():
                push(qa.at[z], qa.at[z], a_send.at[0, 0, 0], q_recv.at[z], me).wait_recv()

            return carry

        lax.fori_loop(0, nc, step, 0)

    collect(EARLY)
    collect(LATE)

    sources = 2
    block = sources * rows
    size = count // PIECES
    factor = 0.25 / math.log(2.0)
    query_length = lengths_ref[cb, 0]

    def keys(i):
        span = slice(i * size, (i + 1) * size)
        return jnp.concatenate([kva[span, :], aux[span, :]], axis=1)

    def give_back(z, rb):
        return push(co.at[z], back.at[rb, zi], c_send.at[z], c_recv.at[rb, zi], at(seg, x, cb * nc + z % nc, zh, y))

    def returned(rb, h):
        push(back.at[rb, h], back.at[rb, h], c_send.at[0], c_recv.at[rb, h], me).wait_recv()

    def attend(s, carry):
        turn = s // (nc // 2)
        first = (cb + turn) % 2 * nc + s % (nc // 2) * 2
        rb = 1 - turn
        parts = []
        for e in range(sources):
            packed = qa[first + e].astype(F32)
            parts += [merge(packed, jnp.zeros_like(packed)), merge(swap(packed), jnp.zeros_like(packed))]
        query = jnp.concatenate(parts, axis=0).astype(BF)
        flag = (lax.broadcasted_iota(jnp.int32, (block, LANES), 1) == 0).astype(BF)
        query = jnp.concatenate([query, flag], axis=1)
        top = None
        for i in range(PIECES):
            piece = lax.dot_general(query, keys(i), (((1,), (1,)), ((), ())), preferred_element_type=F32)
            scores[:, i * size:(i + 1) * size] = piece
            high = jnp.max(piece, axis=1, keepdims=True)
            top = high if top is None else jnp.maximum(top, high)
        shift = top * factor
        acc = None
        for i in range(PIECES):
            weight = jnp.exp2(scores[:, i * size:(i + 1) * size] * factor - shift).astype(BF)
            piece = jnp.dot(weight, keys(i), preferred_element_type=F32)
            acc = piece if acc is None else acc + piece
        context = acc[:, :LANES] / acc[:, LANES + 1:LANES + 2]
        position = (x * NZ + first) * rows + lax.broadcasted_iota(jnp.int32, (block, LANES), 0)
        context = jnp.where(position < query_length, context, 0.0)
        for e in range(sources):
            low = context[2 * e * half:(2 * e + 1) * half]
            high = context[(2 * e + 1) * half:(2 * e + 2) * half]
            z = first + e
            co[z] = merge(swap(low), high).astype(BF)

            @pl.when(z % nc != zi)
            def _():
                give_back(z, rb).start()

            @pl.when(z % nc == zi)
            def _():
                back[rb, zi] = co[z]

        @pl.when(s == nc // 2)
        def _():
            multiply(LATE)

        return carry

    def y_copy(rb, k):
        yy = (y + k) % NY
        return push(part.at[rb, yy], landed.at[rb, y], y_send.at[rb, k], y_recv.at[rb, y], at(seg, x, zl, zh, yy))

    def multiply(rb):
        for k in range(1, nc):
            returned(rb, (zi + k) % nc)
        for t in range(heads // 2):
            even = back[rb, 2 * t].astype(F32)
            odd = back[rb, 2 * t + 1].astype(F32)
            tile = slice(t * LANES, (t + 1) * LANES)
            full[:half, tile] = merge(even, swap(odd)).astype(BF)
            full[half:, tile] = merge(swap(even), odd).astype(BF)

        def projected(zz, yy):
            cols = pl.ds(pl.multiple_of((zz * NY + yy) * chunk, chunk), chunk)
            return jnp.dot(full[...], wo[:, cols], preferred_element_type=F32)

        for k in range(1, NY):
            yy = (y + k) % NY
            for zz in range(NH):
                part[rb, yy, zz] = projected(zz, yy).astype(BF)
            y_copy(rb, k).start()
        for zz in range(NH):
            own[rb, zz] = projected(zz, y)

    def add_up(rb):
        for k in range(1, NY):
            yy = (y + NY - k) % NY
            push(landed.at[rb, yy], landed.at[rb, yy], y_send.at[0, 0], y_recv.at[rb, yy], me).wait_recv()
            for zz in range(NH):
                own[rb, zz] += landed[rb, yy, zz].astype(F32)

    def home(i):
        device = [at(seg, x, zl, far, y), at(seg, x, z4, zh, y), at(seg, x, z4, far, y)][i]
        return push(fs.at[i], fin.at[i], e_send.at[i], e_recv.at[i], device)

    loads[4].wait()
    lax.fori_loop(0, nc, attend, 0)
    add_up(LATE)
    fs[0] = own[LATE, far].astype(BF)
    home(0).start()
    multiply(EARLY)
    add_up(EARLY)
    fs[2] = own[EARLY, far].astype(BF)
    home(2).start()
    fs[1] = own[EARLY, zh].astype(BF)
    home(1).start()
    home(0).wait()
    out_ref[cb] = (hv[cb].astype(F32) + own[LATE, zh] + fin[0].astype(F32)).astype(BF)
    home(1).wait()
    home(2).wait()
    out_ref[1 - cb] = (hv[1 - cb].astype(F32) + fin[1].astype(F32) + fin[2].astype(F32)).astype(BF)

    for copy in spread(0, h_ref):
        copy.wait_send()

    @pl.when(seg == 0)
    def _():
        for copy in spread(1, m_ref):
            copy.wait_send()

    for rb in (EARLY, LATE):
        for c in (mp, omp):
            for copy in along_y(0, rb, c):
                copy.wait_send()

            @pl.when(seg == 1)
            def _():
                for copy in along_y(1, rb, c):
                    copy.wait_send()

        for k in range(1, nc):
            for copy in exchange(rb, k):
                copy.wait_send()
        for k in range(1, NY):
            y_copy(rb, k).wait_send()

    def drain(z, carry):
        for k in range(1, NX):
            along_x(z, k).wait_send()

        @pl.when(z % nc != zi)
        def _():
            give_back(z, 0).wait_send()

        return carry

    lax.fori_loop(0, NZ, drain, 0)


def layer(lengths, hidden, memory, w_query, w_key, w_value, w_out, norm_gain, final_gain):
    batch, rows, chunk = hidden.shape
    depth, cols = w_query.shape
    count = NX * NZ * rows
    parts = NH * NY
    nc = NZ // 2
    dma = pltpu.SemaphoreType.DMA
    vmem = pl.BlockSpec(memory_space=pltpu.VMEM)
    hbm = pl.BlockSpec(memory_space=pltpu.HBM)
    smem = pl.BlockSpec(memory_space=pltpu.SMEM)
    return pl.pallas_call(
        layer_kernel,
        out_shape=jax.ShapeDtypeStruct((batch, rows, chunk), BF),
        in_specs=[smem] + [hbm] * 6 + [vmem] * 2,
        out_specs=vmem,
        scratch_shapes=[
            pltpu.VMEM((batch, rows, chunk), BF),
            pltpu.VMEM((depth, cols), BF),
            pltpu.VMEM((depth, cols), BF),
            pltpu.VMEM((depth, cols), BF),
            pltpu.VMEM((cols, depth), BF),
            pltpu.VMEM((2, depth), F32),
            pltpu.VMEM((2, 2, parts, rows, chunk), BF),
            pltpu.VMEM((2, rows, cols), F32),
            pltpu.VMEM((2, rows, cols), F32),
            pltpu.VMEM((2, rows, cols), F32),
            pltpu.VMEM((2, 2, rows, LANES), F32),
            pltpu.VMEM((2, nc, rows // 2, LANES), BF),
            pltpu.VMEM((2, nc, rows, LANES), BF),
            pltpu.VMEM((NZ, rows // 2, LANES), BF),
            pltpu.VMEM((count, LANES), BF),
            pltpu.VMEM((count, LANES), BF),
            pltpu.VMEM((2 * rows, count), F32),
            pltpu.VMEM((NZ, rows // 2, LANES), BF),
            pltpu.VMEM((2, nc, rows // 2, LANES), BF),
            pltpu.VMEM((rows, cols), BF),
            pltpu.VMEM((2, NY, NH, rows, chunk), BF),
            pltpu.VMEM((2, NH, rows, chunk), F32),
            pltpu.VMEM((2, NY, NH, rows, chunk), BF),
            pltpu.VMEM((3, rows, chunk), BF),
            pltpu.VMEM((3, rows, chunk), BF),
            dma((5,)),
            dma((2, 4)),
            dma((2, 4, NY)),
            dma((2, 2, parts)),
            dma((2, 2, nc)),
            dma((NZ,)),
            dma((NX, NZ)),
            dma((NZ, NX)),
            dma((NZ,)),
            dma((2, nc)),
            dma((2, NY)),
            dma((2, NY)),
            dma((3,)),
            dma((3,)),
        ],
        compiler_params=pltpu.CompilerParams(
            collective_id=1, has_side_effects=True, vmem_limit_bytes=VMEM_LIMIT
        ),
        name="layer",
    )(lengths, hidden, memory, w_query, w_key, w_value, w_out, norm_gain, final_gain)


def body(hidden, memory, w_query, w_key, w_value, w_out, norm_gain, final_gain, lengths):
    out = layer(
        lengths[0], hidden[0], memory[0], w_query[0], w_key[0], w_value[0], w_out[0],
        norm_gain, final_gain.reshape(norm_gain.shape),
    )
    return out[None]


def solution(mesh):
    return jax.shard_map(
        body,
        mesh=mesh,
        in_specs=(
            P("segment", None, "seq", "mp"),
            P("segment", None, "seq", "mp"),
            P("segment", None, "mp"),
            P("segment", None, "mp"),
            P("segment", None, "mp"),
            P("segment", "mp", None),
            P("segment", None),
            P(),
            P("segment", None, None),
        ),
        out_specs=P("segment", None, "seq", "mp"),
        check_vma=False,
    )
```

time: 835 us -> 112 us (0.13)
  the two profiles are of different devices: /device:TPU:6 before, /device:TPU:1 now
where the time goes in v2:
time: 112 us
  Pallas kernels  110 us (98%)
  local copies, waits for them, and re-layouts  1.59 us (1%)
    pallas_call x1, Pallas kernels, layer(): pl.pallas_call(layer_kernel, out_shape=jax.ShapeDtypeStruct((batch, rows,...  110 us

profile of v2, /device:TPU:1, one launch (start us, length us, event | category | flops | bytes accessed | tf_op | source)
XLA Modules:
  0.0 112.1 jit_solution(11760104046097415770)
XLA Ops:
  0.0 110.5 %layer.1 = bf16[2,160,256]{2,1,0:T(8,128)(2,1)} custom-call(s32[2,2]{1,0:T(2,128)} %bitcast.17, bf16[2,160,256]{2,1,0:T(8,128)(2,1)} %bitcast.14, bf16[2,160,256]{2,1,0:T(8,128)(2,1)} %bitcast.15, bf16[2048,256]{1,0:T(8,128)(2,1)} %bitcast.9, bf16[2048,256]{1,0:T(8,128)(2,1)} %bitcast.10, bf16[2048,256]{1,0:T(8,128)(2,1)} %bitcast.11, ...), custom_call_target="tpu_custom_call" | custom-call | tf_op jit(solution)/shard_map/layer/pallas_call | solution.py:436
  110.5 1.6 %copy.11 = bf16[1,2,160,256]{3,2,1,0:T(8,128)(2,1)} copy(bf16[1,2,160,256]{3,2,1,0:T(8,128)(2,1)} %bitcast.13) | data formatting | bytes 327680

commit v3 on v2

v3 whole, which is shorter than its diff:
```python
import math

import jax
import jax.numpy as jnp
from jax import lax
from jax.experimental import pallas as pl
from jax.experimental.pallas import tpu as pltpu
from jax.sharding import PartitionSpec as P

DH = 64
NX, NZ, NH, NY = 4, 8, 2, 4
PIECES = 5
LANES = 128
BF = jnp.bfloat16
F32 = jnp.float32
VMEM_LIMIT = 60 * 1024 * 1024
NHF = 2
EARLY, LATE = 0, 1


def place():
    seg, seq, mp = lax.axis_index("segment"), lax.axis_index("seq"), lax.axis_index("mp")
    return seg, seq // NZ, seq % NZ, mp // NY, mp % NY


def at(seg, x, zl, zh, y):
    return (seg, x * NZ + zl, zh * NY + y)


def push(src, dst, send, recv, device):
    return pltpu.make_async_remote_copy(
        src_ref=src, dst_ref=dst, send_sem=send, recv_sem=recv,
        device_id=device, device_id_type=pl.DeviceIdType.MESH,
    )


def swap(tile):
    return pltpu.roll(tile, DH, 1)


def merge(low, high):
    return jnp.where(lax.broadcasted_iota(jnp.int32, low.shape, 1) < DH, low, high)


def layer_kernel(
    lengths_ref, h_ref, m_ref, wq_hbm, wk_hbm, wv_hbm, wo_hbm, norm_ref, final_ref,
    out_ref,
    hv, wq, wk, wv, wo, gain, xs, accq, acck, accv, ssq, qs, kvs, qa, kva, aux, scores, tops, sums,
    co, back, full, part, own, landed, fs, fin,
    local, z_send, f_send, x_recv, a_send, q_recv, kv_recv, xf_send, c_send, c_recv, y_send, y_recv,
    e_send, e_recv,
):
    seg, x, zl, zh, y = place()
    nc = NZ // 2
    cb, zi = zl // nc, zl % nc
    z4 = (zl + nc) % NZ
    far = NH - 1 - zh
    mp, omp = zh * NY + y, far * NY + y
    batch, rows, chunk = hv.shape
    half = rows // 2
    heads = nc
    width = chunk * NH * NY
    group = NX * nc * rows
    me = at(seg, x, zl, zh, y)

    barrier = pltpu.get_barrier_semaphore()
    partners = [at(seg, x, zl, far, y), at(seg, x, z4, zh, y), at(seg, x, z4, far, y)]
    partners += [at(1 - seg, x, a, b, y) for a, b in [(zl, zh), (zl, far), (z4, zh), (z4, far)]]
    partners += [at(seg, x, zl, zh, (y + k) % NY) for k in range(1, NY)]
    partners += [at(seg, x, cb * nc + (zi + k) % nc, zh, y) for k in range(1, nc)]
    partners += [at(seg, (x + k) % NX, zl, zh, y) for k in range(1, NX)]
    for device in partners:
        pl.semaphore_signal(barrier, inc=1, device_id=device, device_id_type=pl.DeviceIdType.MESH)

    loads = [
        pltpu.make_async_copy(src, dst, local.at[i])
        for i, (src, dst) in enumerate(
            [(h_ref, hv), (wq_hbm, wq), (wk_hbm, wk), (wv_hbm, wv), (wo_hbm, wo)]
        )
    ]
    for load in loads:
        load.start()

    pl.semaphore_wait(barrier, len(partners))

    def piece(ref, hf):
        return ref.at[pl.ds(hf * (rows // NHF), rows // NHF)]

    def spread(array, src, rb):
        to = array if array else seg
        if rb == EARLY:
            targets = [at(to, x, z4, zh, y), at(to, x, z4, far, y)]
        else:
            targets = [at(to, x, zl, far, y)]
        return [
            push(piece(src.at[(cb + 1 - rb) % 2], hf), piece(xs.at[array, rb, mp], hf),
                 z_send.at[array, 2 * rb + i, hf], x_recv.at[array, rb, mp, hf], d)
            for hf in range(NHF) for i, d in enumerate(targets)
        ]

    def next_door():
        return [
            push(piece(m_ref.at[cb], hf), piece(xs.at[1, LATE, mp], hf), z_send.at[1, 3, hf],
                 x_recv.at[1, LATE, mp, hf], at(1, x, zl, zh, y))
            for hf in range(NHF)
        ]

    def arrived(array, rb, c, hf):
        spot = piece(xs.at[array, rb, c], hf)
        push(spot, spot, f_send.at[0, 0, 0, 0], x_recv.at[array, rb, c, hf], me).wait_recv()

    def along_y(array, rb, c, hf):
        slot = rb * NH + (0 if c is mp else 1)
        spot = piece(xs.at[array, rb, c], hf)
        return [
            push(spot, spot, f_send.at[array, slot, k, hf], x_recv.at[array, rb, c, hf],
                 at(seg, x, zl, zh, (y + k) % NY))
            for k in range(1, NY)
        ]

    def forward(array, rb, c, hf, wait=True):
        if wait:
            arrived(array, rb, c, hf)
        for copy in along_y(array, rb, c, hf):
            copy.start()

    def both(rb, c, hf):
        forward(0, rb, c, hf)

        @pl.when(seg == 1)
        def _():
            forward(1, rb, c, hf)

    @pl.when(seg == 0)
    def _():
        for copy in next_door() + spread(1, m_ref, EARLY):
            copy.start()

    for copy in spread(0, h_ref, EARLY):
        copy.start()

    @pl.when(seg == 0)
    def _():
        for copy in spread(1, m_ref, LATE):
            copy.start()

    for copy in spread(0, h_ref, LATE):
        copy.start()

    loads[0].wait()
    xs[0, LATE, mp] = hv[cb]
    for hf in range(NHF):
        forward(0, LATE, mp, hf, wait=False)

    @pl.when(seg == 1)
    def _():
        for hf in range(NHF):
            forward(1, LATE, mp, hf)

    key_length = lengths_ref[cb, 1]

    def fill(i, carry):
        span = pl.ds(pl.multiple_of(i * rows, rows), rows)
        first = ((i // nc) % NX * NZ + i // (NX * nc) * nc + i % nc) * rows
        row = first + lax.broadcasted_iota(jnp.int32, (rows, LANES), 0)
        lane = lax.broadcasted_iota(jnp.int32, (rows, LANES), 1)
        bias = jnp.where(row < key_length, 0.0, -1e30)
        aux[span, :] = jnp.where(lane == 0, bias, jnp.where(lane == 1, 1.0, 0.0)).astype(BF)
        return carry

    lax.fori_loop(0, NX * NZ, fill, 0)
    accq[...] = jnp.zeros_like(accq)
    acck[...] = jnp.zeros_like(acck)
    accv[...] = jnp.zeros_like(accv)
    ssq[...] = jnp.zeros_like(ssq)
    gain[0:1, :] = norm_ref[...]
    gain[1:2, :] = jnp.where(seg == 0, norm_ref[...], final_ref[...])
    for load in loads[1:4]:
        load.wait()

    def squares(values):
        values = values * values
        return sum(values[:, i * LANES:(i + 1) * LANES] for i in range(chunk // LANES))

    def absorb(rb, first, last):
        def step(j, carry):
            c = (zh + j // NY) % NH * NY + (y + j % NY) % NY

            @pl.when(j % NY > 0)
            def _():
                for hf in range(NHF):
                    arrived(0, rb, c, hf)

                @pl.when(seg == 1)
                def _():
                    for hf in range(NHF):
                        arrived(1, rb, c, hf)

            cols = pl.ds(pl.multiple_of(c * chunk, chunk), chunk)
            xq = xs[0, rb, c].astype(F32)
            ssq[0, rb] += squares(xq)
            accq[rb] += jnp.dot((xq * gain[0:1, cols]).astype(BF), wq[cols, :], preferred_element_type=F32)
            xk = xs[seg, rb, c].astype(F32)
            ssq[1, rb] += squares(xk)
            xk = (xk * gain[1:2, cols]).astype(BF)
            acck[rb] += jnp.dot(xk, wk[cols, :], preferred_element_type=F32)
            accv[rb] += jnp.dot(xk, wv[cols, :], preferred_element_type=F32)
            return carry

        lax.fori_loop(first, last, step, 0)

    zpos = [z4, zl]

    def kv_slot(xx, z):
        return pl.ds(pl.multiple_of(((z // nc * NX + xx) * nc + z % nc) * rows, rows), rows)

    def exchange(rb, k):
        h = (zi + k) % nc
        device = at(seg, x, cb * nc + h, zh, y)
        z = zpos[rb]
        return (
            push(kvs.at[rb, h], kva.at[kv_slot(x, z)], a_send.at[rb, 0, k], kv_recv.at[x, z], device),
            push(qs.at[rb, h], qa.at[z], a_send.at[rb, 1, k], q_recv.at[z], device),
        )

    def along_x(z, k):
        spot = kva.at[kv_slot(x, z)]
        return push(spot, spot, xf_send.at[z, k], kv_recv.at[x, z], at(seg, (x + k) % NX, zl, zh, y))

    def kv_arrived(xx, z):
        spot = kva.at[kv_slot(xx, z)]
        push(spot, spot, xf_send.at[0, 0], kv_recv.at[xx, z], me).wait_recv()

    def q_arrived(z):
        push(qa.at[z], qa.at[z], a_send.at[0, 0, 0], q_recv.at[z], me).wait_recv()

    def project(rb):
        rq = lax.rsqrt(jnp.sum(ssq[0, rb], axis=1, keepdims=True) / width + 1e-06)
        rk = lax.rsqrt(jnp.sum(ssq[1, rb], axis=1, keepdims=True) / width + 1e-06)
        for t in range(heads // 2):
            tile = slice(t * LANES, (t + 1) * LANES)
            k = acck[rb, :, tile] * rk
            v = accv[rb, :, tile] * rk
            q = accq[rb, :, tile] * rq
            kvs[rb, 2 * t] = merge(k, swap(v)).astype(BF)
            kvs[rb, 2 * t + 1] = merge(swap(k), v).astype(BF)
            qs[rb, 2 * t] = merge(q[:half], swap(q[half:])).astype(BF)
            qs[rb, 2 * t + 1] = merge(swap(q[:half]), q[half:]).astype(BF)
        for k in range(1, nc):
            for copy in exchange(rb, k):
                copy.start()
        kva[kv_slot(x, zpos[rb]), :] = kvs[rb, zi]
        qa[zpos[rb]] = qs[rb, zi]

    def origin(rb):
        return (cb + 1 - rb) % 2 * nc

    def from_z(rb, k):
        return origin(rb) + (zi + nc - k) % nc

    def pass_x(rb, k):
        z = from_z(rb, k)

        @pl.when(k > 0)
        def _():
            kv_arrived(x, z)

        for i in range(1, NX):
            along_x(z, i).start()

    def pass_early(k, carry):
        pass_x(EARLY, k)
        return carry

    def collect(rb):
        def step(k, carry):
            for i in range(1, NX):
                kv_arrived((x + i) % NX, from_z(rb, k))
            return carry

        lax.fori_loop(0, nc, step, 0)

    def collect_queries(rb):
        for k in range(1, nc):
            q_arrived(from_z(rb, k))

    absorb(LATE, 0, 1)
    absorb(LATE, 1, NY)
    for hf in range(NHF):
        both(EARLY, mp, hf)
        both(EARLY, omp, hf)
    absorb(EARLY, 0, NH * NY)
    project(EARLY)
    for hf in range(NHF):
        both(LATE, omp, hf)
    lax.fori_loop(0, nc, pass_early, 0)
    absorb(LATE, NY, NH * NY)
    project(LATE)

    block = nc * half
    size = group // PIECES
    factor = 0.25 / math.log(2.0)
    query_length = lengths_ref[cb, 0]

    def keys(rb, i):
        span = pl.ds(pl.multiple_of((cb + 1 - rb) % 2 * group + i * size, size), size)
        return jnp.concatenate([kva[span, :], aux[span, :]], axis=1)

    def weigh(rb, hf, key_block):
        parts = []
        for i in range(nc):
            packed = qa[origin(rb) + i].astype(F32)
            packed = jnp.where(hf == 0, packed, swap(packed))
            parts.append(merge(packed, jnp.zeros_like(packed)))
        query = jnp.concatenate(parts, axis=0).astype(BF)
        flag = (lax.broadcasted_iota(jnp.int32, (block, LANES), 1) == 0).astype(BF)
        query = jnp.concatenate([query, flag], axis=1)
        top = None
        for i in range(PIECES):
            score = lax.dot_general(query, keys(key_block, i), (((1,), (1,)), ((), ())), preferred_element_type=F32)
            scores[:, i * size:(i + 1) * size] = score
            high = jnp.max(score, axis=1, keepdims=True)
            top = high if top is None else jnp.maximum(top, high)
        top = top * factor
        acc = None
        for i in range(PIECES):
            weight = jnp.exp2(scores[:, i * size:(i + 1) * size] * factor - top).astype(BF)
            some = jnp.dot(weight, keys(key_block, i), preferred_element_type=F32)
            acc = some if acc is None else acc + some
        return top, acc

    def begin(s, carry):
        pass_x(LATE, s)

        @pl.when(s == 0)
        def _():
            collect(EARLY)
            collect_queries(EARLY)

        @pl.when(s == 2)
        def _():
            collect_queries(LATE)

        top, acc = weigh(s // 2, s % 2, EARLY)
        tops[s] = jnp.broadcast_to(top, (block, LANES))
        sums[s] = acc
        return carry

    def give_back(t, i):
        return push(co.at[t, i], back.at[t, zi], c_send.at[t, i], c_recv.at[t, zi], at(seg, x, cb * nc + i, zh, y))

    def complete(t, carry):
        rb, hf = 1 - t // 2, t % 2
        s = rb * 2 + hf
        top, acc = weigh(rb, hf, LATE)
        old = tops[s][:, :1]
        new = jnp.maximum(top, old)
        acc = acc * jnp.exp2(top - new) + sums[s] * jnp.exp2(old - new)
        context = acc[:, :LANES] / acc[:, LANES + 1:LANES + 2]
        for i in range(nc):
            position = (x * NZ + origin(rb) + i) * rows + hf * half
            position = position + lax.broadcasted_iota(jnp.int32, (half, LANES), 0)
            kept = jnp.where(position < query_length, context[i * half:(i + 1) * half], 0.0)
            co[t, i] = kept.astype(BF)

            @pl.when(zi != i)
            def _():
                give_back(t, i).start()

            @pl.when(zi == i)
            def _():
                back[t, zi] = co[t, i]

        @pl.when(t > 0)
        def _():
            multiply(t - 1)

        @pl.when(t > 1)
        def _():
            add_up(t - 2)

        return carry

    def y_copy(t, k):
        yy = (y + k) % NY
        return push(part.at[t, yy], landed.at[t, y], y_send.at[t, k], y_recv.at[t, y], at(seg, x, zl, zh, yy))

    def multiply(t):
        for k in range(1, nc):
            h = (zi + k) % nc
            push(back.at[t, h], back.at[t, h], c_send.at[0, 0], c_recv.at[t, h], me).wait_recv()
        for i in range(heads // 2):
            even = back[t, 2 * i].astype(F32)
            odd = back[t, 2 * i + 1].astype(F32)
            full[:, i * LANES:(i + 1) * LANES] = merge(swap(even), odd).astype(BF)

        def projected(zz, yy):
            cols = pl.ds(pl.multiple_of((zz * NY + yy) * chunk, chunk), chunk)
            return jnp.dot(full[...], wo[:, cols], preferred_element_type=F32)

        for k in range(1, NY):
            yy = (y + k) % NY
            for zz in range(NH):
                part[t, yy, zz] = projected(zz, yy).astype(BF)
            y_copy(t, k).start()
        for zz in range(NH):
            own[t, zz] = projected(zz, y)

    def home(i, hf):
        device = [at(seg, x, zl, far, y), at(seg, x, z4, zh, y), at(seg, x, z4, far, y)][i]
        return push(fs.at[i, hf], fin.at[i, hf], e_send.at[i, hf], e_recv.at[i, hf], device)

    def add_up(t):
        hf = t % 2
        for k in range(1, NY):
            yy = (y + NY - k) % NY
            push(landed.at[t, yy], landed.at[t, yy], y_send.at[0, 0], y_recv.at[t, yy], me).wait_recv()
            for zz in range(NH):
                own[t, zz] += landed[t, yy, zz].astype(F32)

        @pl.when(t < 2)
        def _():
            fs[0, hf] = own[t, far].astype(BF)
            home(0, hf).start()

        @pl.when(t >= 2)
        def _():
            fs[2, hf] = own[t, far].astype(BF)
            home(2, hf).start()
            fs[1, hf] = own[t, zh].astype(BF)
            home(1, hf).start()

    lax.fori_loop(0, 4, begin, 0)
    collect(LATE)
    loads[4].wait()
    lax.fori_loop(0, 4, complete, 0)
    multiply(3)
    add_up(2)
    add_up(3)
    for hf in range(2):
        span = slice(hf * half, (hf + 1) * half)
        home(0, hf).wait()
        out_ref[cb, span] = (hv[cb, span].astype(F32) + own[hf, zh] + fin[0, hf].astype(F32)).astype(BF)
    for hf in range(2):
        span = slice(hf * half, (hf + 1) * half)
        home(1, hf).wait()
        home(2, hf).wait()
        out_ref[1 - cb, span] = (
            hv[1 - cb, span].astype(F32) + fin[1, hf].astype(F32) + fin[2, hf].astype(F32)
        ).astype(BF)

    for copy in spread(0, h_ref, EARLY) + spread(0, h_ref, LATE):
        copy.wait_send()

    @pl.when(seg == 0)
    def _():
        for copy in spread(1, m_ref, EARLY) + spread(1, m_ref, LATE) + next_door():
            copy.wait_send()

    for rb in (EARLY, LATE):
        for c in (mp, omp):
            for hf in range(NHF):
                for copy in along_y(0, rb, c, hf):
                    copy.wait_send()

                @pl.when(seg == 1)
                def _():
                    for copy in along_y(1, rb, c, hf):
                        copy.wait_send()

        for k in range(1, nc):
            for copy in exchange(rb, k):
                copy.wait_send()

    def drain(t, carry):
        for k in range(1, NY):
            y_copy(t, k).wait_send()
        for i in range(nc):
            @pl.when(zi != i)
            def _():
                give_back(t, i).wait_send()

        return carry

    lax.fori_loop(0, 4, drain, 0)

    def drain_x(z, carry):
        for k in range(1, NX):
            along_x(z, k).wait_send()
        return carry

    lax.fori_loop(0, NZ, drain_x, 0)


def layer(lengths, hidden, memory, w_query, w_key, w_value, w_out, norm_gain, final_gain):
    batch, rows, chunk = hidden.shape
    depth, cols = w_query.shape
    count = NX * NZ * rows
    parts = NH * NY
    nc = NZ // 2
    half = rows // 2
    block = nc * half
    dma = pltpu.SemaphoreType.DMA
    vmem = pl.BlockSpec(memory_space=pltpu.VMEM)
    hbm = pl.BlockSpec(memory_space=pltpu.HBM)
    smem = pl.BlockSpec(memory_space=pltpu.SMEM)
    return pl.pallas_call(
        layer_kernel,
        out_shape=jax.ShapeDtypeStruct((batch, rows, chunk), BF),
        in_specs=[smem] + [hbm] * 6 + [vmem] * 2,
        out_specs=vmem,
        scratch_shapes=[
            pltpu.VMEM((batch, rows, chunk), BF),
            pltpu.VMEM((depth, cols), BF),
            pltpu.VMEM((depth, cols), BF),
            pltpu.VMEM((depth, cols), BF),
            pltpu.VMEM((cols, depth), BF),
            pltpu.VMEM((2, depth), F32),
            pltpu.VMEM((2, 2, parts, rows, chunk), BF),
            pltpu.VMEM((2, rows, cols), F32),
            pltpu.VMEM((2, rows, cols), F32),
            pltpu.VMEM((2, rows, cols), F32),
            pltpu.VMEM((2, 2, rows, LANES), F32),
            pltpu.VMEM((2, nc, half, LANES), BF),
            pltpu.VMEM((2, nc, rows, LANES), BF),
            pltpu.VMEM((NZ, half, LANES), BF),
            pltpu.VMEM((count, LANES), BF),
            pltpu.VMEM((count, LANES), BF),
            pltpu.VMEM((block, count // 2), F32),
            pltpu.VMEM((4, block, LANES), F32),
            pltpu.VMEM((4, block, 2 * LANES), F32),
            pltpu.VMEM((4, nc, half, LANES), BF),
            pltpu.VMEM((4, nc, half, LANES), BF),
            pltpu.VMEM((half, cols), BF),
            pltpu.VMEM((4, NY, NH, half, chunk), BF),
            pltpu.VMEM((4, NH, half, chunk), F32),
            pltpu.VMEM((4, NY, NH, half, chunk), BF),
            pltpu.VMEM((3, 2, half, chunk), BF),
            pltpu.VMEM((3, 2, half, chunk), BF),
            dma((5,)),
            dma((2, 4, 2)),
            dma((2, 4, NY, 2)),
            dma((2, 2, parts, 2)),
            dma((2, 2, nc)),
            dma((NZ,)),
            dma((NX, NZ)),
            dma((NZ, NX)),
            dma((4, nc)),
            dma((4, nc)),
            dma((4, NY)),
            dma((4, NY)),
            dma((3, 2)),
            dma((3, 2)),
        ],
        compiler_params=pltpu.CompilerParams(
            collective_id=1, has_side_effects=True, vmem_limit_bytes=VMEM_LIMIT
        ),
        name="layer",
    )(lengths, hidden, memory, w_query, w_key, w_value, w_out, norm_gain, final_gain)


def body(hidden, memory, w_query, w_key, w_value, w_out, norm_gain, final_gain, lengths):
    out = layer(
        lengths[0], hidden[0], memory[0], w_query[0], w_key[0], w_value[0], w_out[0],
        norm_gain, final_gain.reshape(norm_gain.shape),
    )
    return out[None]


def solution(mesh):
    return jax.shard_map(
        body,
        mesh=mesh,
        in_specs=(
            P("segment", None, "seq", "mp"),
            P("segment", None, "seq", "mp"),
            P("segment", None, "mp"),
            P("segment", None, "mp"),
            P("segment", None, "mp"),
            P("segment", "mp", None),
            P("segment", None),
            P(),
            P("segment", None, None),
        ),
        out_specs=P("segment", None, "seq", "mp"),
        check_vma=False,
    )
```

time: 112 us -> 103 us (0.920)
  the two profiles are of different devices: /device:TPU:1 before, /device:TPU:6 now
where the time goes in v3:
time: 103 us; the launch traced here: 102 us
  Pallas kernels  101 us (98%)
  local copies, waits for them, and re-layouts  1.59 us (2%)
    pallas_call x1, Pallas kernels, layer(): pl.pallas_call(layer_kernel, out_shape=jax.ShapeDtypeStruct((batch, rows,...  101 us

profile of v3, /device:TPU:6, one launch (start us, length us, event | category | flops | bytes accessed | tf_op | source)
XLA Modules:
  0.0 102.2 jit_solution(16025211642222565720)
XLA Ops:
  0.0 100.6 %layer.1 = bf16[2,160,256]{2,1,0:T(8,128)(2,1)} custom-call(s32[2,2]{1,0:T(2,128)} %bitcast.17, bf16[2,160,256]{2,1,0:T(8,128)(2,1)} %bitcast.14, bf16[2,160,256]{2,1,0:T(8,128)(2,1)} %bitcast.15, bf16[2048,256]{1,0:T(8,128)(2,1)} %bitcast.9, bf16[2048,256]{1,0:T(8,128)(2,1)} %bitcast.10, bf16[2048,256]{1,0:T(8,128)(2,1)} %bitcast.11, ...), custom_call_target="tpu_custom_call" | custom-call | tf_op jit(solution)/shard_map/layer/pallas_call | solution.py:507
  100.6 1.6 %copy.11 = bf16[1,2,160,256]{3,2,1,0:T(8,128)(2,1)} copy(bf16[1,2,160,256]{3,2,1,0:T(8,128)(2,1)} %bitcast.13) | data formatting | bytes 327680

commit v4 on v3

--- a/solution.py
+++ b/solution.py
@@ -371,13 +371,9 @@
             def _():
                 back[t, zi] = co[t, i]
 
-        @pl.when(t > 0)
-        def _():
-            multiply(t - 1)
-
         @pl.when(t > 1)
         def _():
-            add_up(t - 2)
+            multiply(t - 2)
 
         return carry
 
@@ -434,6 +430,9 @@
     collect(LATE)
     loads[4].wait()
     lax.fori_loop(0, 4, complete, 0)
+    add_up(0)
+    multiply(2)
+    add_up(1)
     multiply(3)
     add_up(2)
     add_up(3)

time: 103 us -> 98.8 us (0.959)
  Pallas kernels: 101 us -> 96.1 us
    pallas_call x1, Pallas kernels: 101 us -> 96.1 us  [layer(): pl.pallas_call(layer_kernel, out_shape=jax.ShapeDtypeStruct((batch, rows,...]
where the time goes in v4:
time: 98.8 us; the launch traced here: 97.7 us
  Pallas kernels  96.1 us (97%)
  local copies, waits for them, and re-layouts  1.59 us (2%)
    pallas_call x1, Pallas kernels, layer(): pl.pallas_call(layer_kernel, out_shape=jax.ShapeDtypeStruct((batch, rows,...  96.1 us

profile of v4, /device:TPU:6, one launch (start us, length us, event | category | flops | bytes accessed | tf_op | source)
XLA Modules:
  0.0 97.7 jit_solution(7105541615219012715)
XLA Ops:
  0.0 96.1 %layer.1 = bf16[2,160,256]{2,1,0:T(8,128)(2,1)} custom-call(s32[2,2]{1,0:T(2,128)} %bitcast.17, bf16[2,160,256]{2,1,0:T(8,128)(2,1)} %bitcast.14, bf16[2,160,256]{2,1,0:T(8,128)(2,1)} %bitcast.15, bf16[2048,256]{1,0:T(8,128)(2,1)} %bitcast.9, bf16[2048,256]{1,0:T(8,128)(2,1)} %bitcast.10, bf16[2048,256]{1,0:T(8,128)(2,1)} %bitcast.11, ...), custom_call_target="tpu_custom_call" | custom-call | tf_op jit(solution)/shard_map/layer/pallas_call | solution.py:506
  96.1 1.6 %copy.11 = bf16[1,2,160,256]{3,2,1,0:T(8,128)(2,1)} copy(bf16[1,2,160,256]{3,2,1,0:T(8,128)(2,1)} %bitcast.13) | data formatting | bytes 327680

commit v5 on v4

--- a/solution.py
+++ b/solution.py
@@ -115,7 +115,7 @@
         return [
             push(spot, spot, f_send.at[array, slot, k, hf], x_recv.at[array, rb, c, hf],
                  at(seg, x, zl, zh, (y + k) % NY))
-            for k in range(1, NY)
+            for k in (2, 1, 3)
         ]
 
     def forward(array, rb, c, hf, wait=True):
@@ -394,7 +394,7 @@
             cols = pl.ds(pl.multiple_of((zz * NY + yy) * chunk, chunk), chunk)
             return jnp.dot(full[...], wo[:, cols], preferred_element_type=F32)
 
-        for k in range(1, NY):
+        for k in (2, 1, 3):
             yy = (y + k) % NY
             for zz in range(NH):
                 part[t, yy, zz] = projected(zz, yy).astype(BF)

time: 98.8 us -> 98.3 us (level)
  no operation moved by 1% of the time
where the time goes in v5:
time: 98.3 us; the launch traced here: 98.1 us
  Pallas kernels  96.5 us (98%)
  local copies, waits for them, and re-layouts  1.59 us (2%)
    pallas_call x1, Pallas kernels, layer(): pl.pallas_call(layer_kernel, out_shape=jax.ShapeDtypeStruct((batch, rows,...  96.5 us

profile of v5, /device:TPU:6, one launch (start us, length us, event | category | flops | bytes accessed | tf_op | source)
XLA Modules:
  0.0 98.1 jit_solution(12492183928578124882)
XLA Ops:
  0.0 96.5 %layer.1 = bf16[2,160,256]{2,1,0:T(8,128)(2,1)} custom-call(s32[2,2]{1,0:T(2,128)} %bitcast.17, bf16[2,160,256]{2,1,0:T(8,128)(2,1)} %bitcast.14, bf16[2,160,256]{2,1,0:T(8,128)(2,1)} %bitcast.15, bf16[2048,256]{1,0:T(8,128)(2,1)} %bitcast.9, bf16[2048,256]{1,0:T(8,128)(2,1)} %bitcast.10, bf16[2048,256]{1,0:T(8,128)(2,1)} %bitcast.11, ...), custom_call_target="tpu_custom_call" | custom-call | tf_op jit(solution)/shard_map/layer/pallas_call | solution.py:506
  96.5 1.6 %copy.11 = bf16[1,2,160,256]{3,2,1,0:T(8,128)(2,1)} copy(bf16[1,2,160,256]{3,2,1,0:T(8,128)(2,1)} %bitcast.13) | data formatting | bytes 327680
